TPU v7x, 512 devices: a whole 4x8x8 slice. The times are simulated.
512 devices in a mesh: seq: 64 (over x, y, core), head: 8 (over z).
Axes of the slice: x: 4, y: 8, z: 8, core: 2. Of those that a mesh axis runs over, the one named last changes fastest.
Arguments:
- query_rows: bfloat16 [8192, 3072], P(('seq', 'head')), may hold values from -5 to 5
- key_rows: bfloat16 [8192, 3072], P(('seq', 'head')), may hold values from -5 to 5
- value_rows: bfloat16 [8192, 3072], P(('seq', 'head')), may hold values from -6 to 6
- out_grad: bfloat16 [8192, 3072], P(('seq', 'head')), may hold values from -6 to 6
- block_mask: int32 [4, 4, 4], replicated, may hold values 0 or 1
Outputs:
- attended: bfloat16 [8192, 3072], P(('seq', 'head'))
- grad_query: bfloat16 [8192, 3072], P(('seq', 'head'))
- grad_keys: bfloat16 [8192, 3072], P(('seq', 'head'))
- grad_values: bfloat16 [8192, 3072], P(('seq', 'head'))
All inputs are finite; a program needn't handle non-finite values.
Results may differ from a plain program's by a relative error of at most 0.024.
Values may be sent and summed in bfloat16 or wider, within the bound.
A program may use at most 64 MiB of HBM per device.

v0:
```python
import math

import jax
import jax.numpy as jnp
from jax import lax
from jax.sharding import PartitionSpec as P

HD = 128
BLOCK = 128
GROUP = 4


def partner_2(shard, axis, distance):
    return lax.ppermute(shard, axis, [(i, i ^ 1 << distance) for i in range(lax.axis_size(axis))])


def passed_along(shard, axis, by):
    peers = lax.axis_size(axis)
    pairs = [(i, i + by) for i in range(peers) if 0 <= i + by < peers]
    return lax.ppermute(shard, axis, pairs)


def widen_mask(bits):
    blocks = bits.shape[0]
    grid = jnp.broadcast_to((bits > 0)[:, None, :, None], (blocks, BLOCK, blocks, BLOCK))
    return grid.reshape(blocks * BLOCK, blocks * BLOCK)


def place_pair(mine, other, is_low, dim):
    return lax.cond(
        is_low,
        lambda pair: jnp.concatenate([pair[0], pair[1]], dim),
        lambda pair: jnp.concatenate([pair[1], pair[0]], dim),
        (mine, other),
    )


def per_device(query_rows, key_rows, value_rows, out_grad, block_mask):
    queries, keys_local, values_local, grads_output = (
        lax.all_to_all(query_rows, "head", split_axis=1, concat_axis=0, tiled=True),
        lax.all_to_all(key_rows, "head", split_axis=1, concat_axis=0, tiled=True),
        lax.all_to_all(value_rows, "head", split_axis=1, concat_axis=0, tiled=True),
        lax.all_to_all(out_grad, "head", split_axis=1, concat_axis=0, tiled=True),
    )
    seq_index = lax.axis_index("seq")
    group_bits = GROUP.bit_length() - 1
    rank = seq_index % GROUP
    frame_index = seq_index // GROUP
    frame_count = lax.axis_size("seq") // GROUP
    level_count = block_mask.shape[0]
    block_rows = queries.shape[0]
    frame_tokens = block_rows * GROUP
    head_count = queries.shape[1] // HD
    score_scale = 1.0 / math.sqrt(HD)
    own_pair = jnp.stack([keys_local, values_local])

    def low_bit(bit):
        return seq_index >> bit & 1 == 0

    whole_pair = own_pair
    for bit in range(group_bits):
        other = partner_2(whole_pair, "seq", bit)
        whole_pair = place_pair(whole_pair, other, low_bit(bit), 1)
    partner_list = []
    for level_index in range(level_count):
        for orient in (1, -1):
            partner_list.append(
                passed_along(whole_pair, "seq", orient * GROUP * (1 << level_index))
            )
    every_pair = jnp.concatenate([whole_pair] + partner_list, axis=1)
    keys_all, values_all = (every_pair[0], every_pair[1])
    allowed_list = [jnp.ones((block_rows, frame_tokens), bool)]
    for level_index in range(level_count):
        for orient in (1, -1):
            partner = frame_index - orient * (1 << level_index)
            inside = (partner >= 0) & (partner < frame_count)
            allowed_list.append(
                lax.dynamic_slice_in_dim(
                    widen_mask(block_mask[level_index]), rank * block_rows, block_rows, 0
                )
                & inside
            )
    allowed = jnp.concatenate(allowed_list, axis=1)

    def head_scores(query_head, keys_head):
        scores = (
            jnp.einsum("qd,kd->qk", query_head, keys_head, preferred_element_type=jnp.float32)
            * score_scale
        )
        return jnp.where(allowed, scores, -jnp.inf)

    outputs = []
    logsums = []
    for head_index in range(head_count):
        columns = slice(head_index * HD, (head_index + 1) * HD)
        scores = head_scores(queries[:, columns], keys_all[:, columns])
        peak = jnp.max(scores, axis=1, keepdims=True)
        logsum = peak + jnp.log(jnp.sum(jnp.exp(scores - peak), axis=1, keepdims=True))
        weights = jnp.exp(scores - logsum).astype(jnp.bfloat16)
        outputs.append(
            jnp.dot(weights, values_all[:, columns], preferred_element_type=jnp.float32).astype(
                jnp.bfloat16
            )
        )
        logsums.append(logsum)
    attended = jnp.concatenate(outputs, axis=1)
    query_grads = []
    key_grads = []
    value_grads = []
    for head_index in range(head_count):
        columns = slice(head_index * HD, (head_index + 1) * HD)
        query_head = queries[:, columns]
        grad_head = grads_output[:, columns]
        scores = head_scores(query_head, keys_all[:, columns])
        probability = jnp.exp(scores - logsums[head_index])
        weights = probability.astype(jnp.bfloat16)
        grad_weights = jnp.einsum(
            "qd,kd->qk", grad_head, values_all[:, columns], preferred_element_type=jnp.float32
        )
        delta_row = jnp.sum(
            grad_head.astype(jnp.float32) * attended[:, columns].astype(jnp.float32),
            axis=1,
            keepdims=True,
        )
        grad_scores = (probability * (grad_weights - delta_row) * score_scale).astype(jnp.bfloat16)
        query_grads.append(
            jnp.dot(grad_scores, keys_all[:, columns], preferred_element_type=jnp.float32).astype(
                jnp.bfloat16
            )
        )
        key_grads.append(
            jnp.einsum(
                "qk,qd->kd", grad_scores, query_head, preferred_element_type=jnp.float32
            ).astype(jnp.bfloat16)
        )
        value_grads.append(
            jnp.einsum("qk,qd->kd", weights, grad_head, preferred_element_type=jnp.float32).astype(
                jnp.bfloat16
            )
        )
    grad_query = jnp.concatenate(query_grads, axis=1)
    grad_pair = jnp.stack(
        [jnp.concatenate(key_grads, axis=1), jnp.concatenate(value_grads, axis=1)]
    )
    total = grad_pair[:, :frame_tokens].astype(jnp.float32)
    piece_index = 1
    for level_index in range(level_count):
        for orient in (1, -1):
            piece = grad_pair[:, piece_index * frame_tokens : (piece_index + 1) * frame_tokens]
            returned = passed_along(piece, "seq", -orient * GROUP * (1 << level_index))
            total = total + returned.astype(jnp.float32)
            piece_index += 1
    for bit in reversed(range(group_bits)):
        half = total.shape[1] // 2
        first_half = total[:, :half]
        second_half = total[:, half:]
        is_low = low_bit(bit)
        outgoing = jnp.where(is_low, second_half, first_half)
        staying = jnp.where(is_low, first_half, second_half)
        total = staying + partner_2(outgoing, "seq", bit)
    grad_keys = total[0].astype(jnp.bfloat16)
    grad_values = total[1].astype(jnp.bfloat16)
    return (
        lax.all_to_all(attended, "head", split_axis=0, concat_axis=1, tiled=True),
        lax.all_to_all(grad_query, "head", split_axis=0, concat_axis=1, tiled=True),
        lax.all_to_all(grad_keys, "head", split_axis=0, concat_axis=1, tiled=True),
        lax.all_to_all(grad_values, "head", split_axis=0, concat_axis=1, tiled=True),
    )


def solution(mesh):
    placed = (
        P(("seq", "head"), None),
        P(("seq", "head"), None),
        P(("seq", "head"), None),
        P(("seq", "head"), None),
        P(),
    )
    return jax.shard_map(
        per_device,
        mesh=mesh,
        in_specs=placed,
        out_specs=(
            P(("seq", "head"), None),
            P(("seq", "head"), None),
            P(("seq", "head"), None),
            P(("seq", "head"), None),
        ),
        check_vma=False,
    )
```

profile of v0, /device:TPU:20, one launch (start us, length us, event | category | flops | bytes accessed | tf_op | source)
XLA Modules:
  0.0 390.4 jit_solution(10142112670236873719)
XLA Ops:
  2.2 10.3 %all-to-all-start.1 = ((bf16[16,8,384]{2,0,1:T(8,128)(2,1)}), bf16[16,8,384]{2,0,1:T(8,128)(2,1)S(1)}, u32[]{:S(2)}, u32[]{:S(2)}) async-start(bf16[16,8,384]{2,0,1:T(8,128)(2,1)} %bitcast.128), calls=%async_computation.1 | async-start | bytes 196608 | tf_op jit(solution)/shard_map/all_to_all | solution.py:42
  14.0 7.2 %all-to-all-done.1 = bf16[16,8,384]{2,0,1:T(8,128)(2,1)S(1)} async-done(((bf16[16,8,384]{2,0,1:T(8,128)(2,1)}), bf16[16,8,384]{2,0,1:T(8,128)(2,1)S(1)}, u32[]{:S(2)}, u32[]{:S(2)}) %all-to-all-start.1) | async-done | bytes 98336 | tf_op jit(solution)/shard_map/all_to_all | solution.py:42
  26.1 7.1 %all-to-all-done = bf16[16,8,384]{2,0,1:T(8,128)(2,1)S(1)} async-done(((bf16[16,8,384]{2,0,1:T(8,128)(2,1)}), bf16[16,8,384]{2,0,1:T(8,128)(2,1)S(1)}, u32[]{:S(2)}, u32[]{:S(2)}) %all-to-all-start) | async-done | bytes 98336 | tf_op jit(solution)/shard_map/all_to_all | solution.py:41
  45.7 7.3 %collective-permute-done.1 = bf16[2,256,384]{2,1,0:T(8,128)(2,1)S(1)} collective-permute-done((bf16[2,256,384]{2,1,0:T(8,128)(2,1)S(1)}, bf16[2,256,384]{2,1,0:T(8,128)(2,1)S(1)}, u32[]{:S(2)}, u32[]{:S(2)}) %collective-permute-start.1) | collective-permute-done | bytes 393248 | tf_op jit(solution)/shard_map/ppermute | solution.py:14
  53.2 5.7 %collective-permute-start.2 = (bf16[2,512,384]{2,1,0:T(8,128)(2,1)S(1)}, bf16[2,512,384]{2,1,0:T(8,128)(2,1)S(1)}, u32[]{:S(2)}, u32[]{:S(2)}) collective-permute-start(bf16[2,512,384]{2,1,0:T(8,128)(2,1)S(1)} %get-tuple-element.68), channel_id=1, source_target_pairs={{0,32},{8,40},{16,48},{24,56},{32,64},{40,72},{48,80},{56,88},{64,... | collective-permute-start | bytes 2359304 | tf_op jit(solution)/shard_map/ppermute | solution.py:20
  62.2 5.0 %collective-permute-start.4 = (bf16[2,512,384]{2,1,0:T(8,128)(2,1)S(1)}, bf16[2,512,384]{2,1,0:T(8,128)(2,1)}, u32[]{:S(2)}, u32[]{:S(2)}) collective-permute-start(bf16[2,512,384]{2,1,0:T(8,128)(2,1)S(1)} %get-tuple-element.68), channel_id=1, source_target_pairs={{0,64},{8,72},{16,80},{24,88},{32,96},{40,104},{48,112},{56,120},{... | collective-permute-start | bytes 2359304 | tf_op jit(solution)/shard_map/ppermute | solution.py:20
  68.5 5.6 %collective-permute-start.5 = (bf16[2,512,384]{2,1,0:T(8,128)(2,1)S(1)}, bf16[2,512,384]{2,1,0:T(8,128)(2,1)}, u32[]{:S(2)}, u32[]{:S(2)}) collective-permute-start(bf16[2,512,384]{2,1,0:T(8,128)(2,1)S(1)} %get-tuple-element.68), channel_id=1, source_target_pairs={{64,0},{72,8},{80,16},{88,24},{96,32},{104,40},{112,48},{120,56},{... | collective-permute-start | bytes 2359304 | tf_op jit(solution)/shard_map/ppermute | solution.py:20
  78.6 7.1 %all-to-all-start.2 = ((bf16[16,8,384]{2,0,1:T(8,128)(2,1)}), bf16[16,8,384]{2,0,1:T(8,128)(2,1)}, u32[]{:S(2)}, u32[]{:S(2)}) async-start(bf16[16,8,384]{2,0,1:T(8,128)(2,1)} %bitcast.127), calls=%async_computation.2 | async-start | bytes 196608 | tf_op jit(solution)/shard_map/all_to_all | solution.py:40
  87.9 12.6 %collective-permute-done.2 = bf16[2,512,384]{2,1,0:T(8,128)(2,1)S(1)} collective-permute-done((bf16[2,512,384]{2,1,0:T(8,128)(2,1)S(1)}, bf16[2,512,384]{2,1,0:T(8,128)(2,1)S(1)}, u32[]{:S(2)}, u32[]{:S(2)}) %collective-permute-start.2) | collective-permute-done | bytes 786464 | tf_op jit(solution)/shard_map/ppermute | solution.py:20
  103.5 62.8 %collective-permute-done.3 = bf16[2,512,384]{2,1,0:T(8,128)(2,1)S(1)} collective-permute-done((bf16[2,512,384]{2,1,0:T(8,128)(2,1)S(1)}, bf16[2,512,384]{2,1,0:T(8,128)(2,1)S(1)}, u32[]{:S(2)}, u32[]{:S(2)}) %collective-permute-start.3) | collective-permute-done | bytes 786464 | tf_op jit(solution)/shard_map/ppermute | solution.py:20
  167.8 6.3 %collective-permute-start.9 = (bf16[2,512,384]{2,1,0:T(8,128)(2,1)S(1)}, bf16[2,512,384]{2,1,0:T(8,128)(2,1)S(1)}, u32[]{:S(2)}, u32[]{:S(2)}) collective-permute-start(bf16[2,512,384]{2,1,0:T(8,128)(2,1)S(1)} %get-tuple-element.68), channel_id=1, source_target_pairs={{256,0},{264,8},{272,16},{280,24},{288,32},{296,40},{304,48},{312,... | collective-permute-start | bytes 2359304 | tf_op jit(solution)/shard_map/ppermute | solution.py:20
  206.3 6.1 %collective-permute-start.16 = (bf16[2,512,384]{1,2,0:T(8,128)(2,1)S(1)}, bf16[2,512,384]{1,2,0:T(8,128)(2,1)S(1)}, u32[]{:S(2)}, u32[]{:S(2)}) collective-permute-start(bf16[2,512,384]{1,2,0:T(8,128)(2,1)S(1)} %get-tuple-element.41), channel_id=1, source_target_pairs={{256,0},{264,8},{272,16},{280,24},{288,32},{296,40},{304,48},{312,... | collective-permute-start | bytes 2359304 | tf_op jit(solution)/shard_map/ppermute | solution.py:20
  220.7 8.3 %collective-permute-start.12 = (bf16[2,512,384]{1,2,0:T(8,128)(2,1)S(1)}, bf16[2,512,384]{1,2,0:T(8,128)(2,1)S(1)}, u32[]{:S(2)}, u32[]{:S(2)}) collective-permute-start(bf16[2,512,384]{1,2,0:T(8,128)(2,1)S(1)} %get-tuple-element.36), channel_id=1, source_target_pairs={{64,0},{72,8},{80,16},{88,24},{96,32},{104,40},{112,48},{120,56},{... | collective-permute-start | bytes 2359304 | tf_op jit(solution)/shard_map/ppermute | solution.py:20
  231.0 4.8 %collective-permute-start.10 = (bf16[2,512,384]{1,2,0:T(8,128)(2,1)S(1)}, bf16[2,512,384]{1,2,0:T(8,128)(2,1)S(1)}, u32[]{:S(2)}, u32[]{:S(2)}) collective-permute-start(bf16[2,512,384]{1,2,0:T(8,128)(2,1)S(1)} %get-tuple-element.34), channel_id=1, source_target_pairs={{32,0},{40,8},{48,16},{56,24},{64,32},{72,40},{80,48},{88,56},{96,... | collective-permute-start | bytes 2359304 | tf_op jit(solution)/shard_map/ppermute | solution.py:20
  235.8 30.0 %collective-permute-done.13 = bf16[2,512,384]{1,2,0:T(8,128)(2,1)S(1)} collective-permute-done((bf16[2,512,384]{1,2,0:T(8,128)(2,1)S(1)}, bf16[2,512,384]{1,2,0:T(8,128)(2,1)S(1)}, u32[]{:S(2)}, u32[]{:S(2)}) %collective-permute-start.13) | collective-permute-done | bytes 786464 | tf_op jit(solution)/shard_map/ppermute | solution.py:20
  265.8 17.1 %collective-permute-done.12 = bf16[2,512,384]{1,2,0:T(8,128)(2,1)S(1)} collective-permute-done((bf16[2,512,384]{1,2,0:T(8,128)(2,1)S(1)}, bf16[2,512,384]{1,2,0:T(8,128)(2,1)S(1)}, u32[]{:S(2)}, u32[]{:S(2)}) %collective-permute-start.12) | collective-permute-done | bytes 786464 | tf_op jit(solution)/shard_map/ppermute | solution.py:20
  283.0 33.7 %collective-permute-done.11 = bf16[2,512,384]{1,2,0:T(8,128)(2,1)S(1)} collective-permute-done((bf16[2,512,384]{1,2,0:T(8,128)(2,1)S(1)}, bf16[2,512,384]{1,2,0:T(8,128)(2,1)S(1)}, u32[]{:S(2)}, u32[]{:S(2)}) %collective-permute-start.11) | collective-permute-done | bytes 786464 | tf_op jit(solution)/shard_map/ppermute | solution.py:20
  316.7 4.3 %collective-permute-done.10 = bf16[2,512,384]{1,2,0:T(8,128)(2,1)S(1)} collective-permute-done((bf16[2,512,384]{1,2,0:T(8,128)(2,1)S(1)}, bf16[2,512,384]{1,2,0:T(8,128)(2,1)S(1)}, u32[]{:S(2)}, u32[]{:S(2)}) %collective-permute-start.10) | collective-permute-done | bytes 786464 | tf_op jit(solution)/shard_map/ppermute | solution.py:20
  328.0 7.1 %all-to-all-start.3 = ((bf16[8,16,384]{2,1,0:T(8,128)(2,1)}), bf16[8,16,384]{2,1,0:T(8,128)(2,1)}, u32[]{:S(2)}, u32[]{:S(2)}) async-start(bf16[8,16,384]{2,1,0:T(8,128)(2,1)} %bitcast.149), calls=%async_computation.3 | async-start | bytes 196608 | tf_op jit(solution)/shard_map/all_to_all | solution.py:164
  338.9 4.8 %collective-permute-done.18 = f32[2,256,384]{1,2,0:T(8,128)} collective-permute-done((f32[2,256,384]{1,2,0:T(8,128)S(1)}, f32[2,256,384]{1,2,0:T(8,128)}, u32[]{:S(2)}, u32[]{:S(2)}) %collective-permute-start.18) | collective-permute-done | bytes 786464 | tf_op jit(solution)/shard_map/ppermute | solution.py:14
  349.5 7.1 %all-to-all-start.5 = ((bf16[8,16,384]{2,1,0:T(8,128)(2,1)}), bf16[8,16,384]{2,1,0:T(8,128)(2,1)S(1)}, u32[]{:S(2)}, u32[]{:S(2)}) async-start(bf16[8,16,384]{2,1,0:T(8,128)(2,1)} %bitcast.24), calls=%async_computation.5 | async-start | bytes 196608 | tf_op jit(solution)/shard_map/all_to_all | solution.py:165
  357.4 8.3 %all-to-all-done.5 = bf16[8,16,384]{2,1,0:T(8,128)(2,1)S(1)} async-done(((bf16[8,16,384]{2,1,0:T(8,128)(2,1)}), bf16[8,16,384]{2,1,0:T(8,128)(2,1)S(1)}, u32[]{:S(2)}, u32[]{:S(2)}) %all-to-all-start.5) | async-done | bytes 98336 | tf_op jit(solution)/shard_map/all_to_all | solution.py:165
  369.8 7.9 %all-to-all-done.6 = bf16[8,16,384]{2,1,0:T(8,128)(2,1)S(1)} async-done(((bf16[8,16,384]{2,1,0:T(8,128)(2,1)}), bf16[8,16,384]{2,1,0:T(8,128)(2,1)S(1)}, u32[]{:S(2)}, u32[]{:S(2)}) %all-to-all-start.6) | async-done | bytes 98336 | tf_op jit(solution)/shard_map/all_to_all | solution.py:166
  383.9 5.8 %all-to-all-done.7 = bf16[8,16,384]{2,1,0:T(8,128)(2,1)S(1)} async-done(((bf16[8,16,384]{2,1,0:T(8,128)(2,1)}), bf16[8,16,384]{2,1,0:T(8,128)(2,1)S(1)}, u32[]{:S(2)}, u32[]{:S(2)}) %all-to-all-start.7) | async-done | bytes 98336 | tf_op jit(solution)/shard_map/all_to_all | solution.py:167
  (149 shorter events, 106.5 us)
Async XLA Ops:
  2.2 19.0 %all-to-all-start.1 = ((bf16[16,8,384]{2,0,1:T(8,128)(2,1)}), bf16[16,8,384]{2,0,1:T(8,128)(2,1)S(1)}, u32[]{:S(2)}, u32[]{:S(2)}) async-start(bf16[16,8,384]{2,0,1:T(8,128)(2,1)} %bitcast.128), calls=%async_computation.1 | async-start | bytes 196608 | tf_op jit(solution)/shard_map/all_to_all | solution.py:42
  33.2 45.3 %all-to-all-start.4 = ((bf16[16,8,384]{2,0,1:T(8,128)(2,1)}), bf16[16,8,384]{2,0,1:T(8,128)(2,1)S(1)}, u32[]{:S(2)}, u32[]{:S(2)}) async-start(bf16[16,8,384]{2,0,1:T(8,128)(2,1)} %bitcast.126), calls=%async_computation.4 | async-start | bytes 196608 | tf_op jit(solution)/shard_map/all_to_all | solution.py:43
  40.0 13.1 %collective-permute-start.1 = (bf16[2,256,384]{2,1,0:T(8,128)(2,1)S(1)}, bf16[2,256,384]{2,1,0:T(8,128)(2,1)S(1)}, u32[]{:S(2)}, u32[]{:S(2)}) collective-permute-start(bf16[2,256,384]{2,1,0:T(8,128)(2,1)S(1)} %get-tuple-element.67), channel_id=1, source_target_pairs={{0,16},{8,24},{16,0},{24,8},{32,48},{40,56},{48,32},{56,40},{64,80... | collective-permute-start | bytes 1179656 | tf_op jit(solution)/shard_map/ppermute | solution.py:14
  53.2 47.3 %collective-permute-start.2 = (bf16[2,512,384]{2,1,0:T(8,128)(2,1)S(1)}, bf16[2,512,384]{2,1,0:T(8,128)(2,1)S(1)}, u32[]{:S(2)}, u32[]{:S(2)}) collective-permute-start(bf16[2,512,384]{2,1,0:T(8,128)(2,1)S(1)} %get-tuple-element.68), channel_id=1, source_target_pairs={{0,32},{8,40},{16,48},{24,56},{32,64},{40,72},{48,80},{56,88},{64,... | collective-permute-start | bytes 2359304 | tf_op jit(solution)/shard_map/ppermute | solution.py:20
  59.6 106.7 %collective-permute-start.3 = (bf16[2,512,384]{2,1,0:T(8,128)(2,1)S(1)}, bf16[2,512,384]{2,1,0:T(8,128)(2,1)S(1)}, u32[]{:S(2)}, u32[]{:S(2)}) collective-permute-start(bf16[2,512,384]{2,1,0:T(8,128)(2,1)S(1)} %get-tuple-element.68), channel_id=1, source_target_pairs={{32,0},{40,8},{48,16},{56,24},{64,32},{72,40},{80,48},{88,56},{96,... | collective-permute-start | bytes 2359304 | tf_op jit(solution)/shard_map/ppermute | solution.py:20
  62.2 105.6 %collective-permute-start.4 = (bf16[2,512,384]{2,1,0:T(8,128)(2,1)S(1)}, bf16[2,512,384]{2,1,0:T(8,128)(2,1)}, u32[]{:S(2)}, u32[]{:S(2)}) collective-permute-start(bf16[2,512,384]{2,1,0:T(8,128)(2,1)S(1)} %get-tuple-element.68), channel_id=1, source_target_pairs={{0,64},{8,72},{16,80},{24,88},{32,96},{40,104},{48,112},{56,120},{... | collective-permute-start | bytes 2359304 | tf_op jit(solution)/shard_map/ppermute | solution.py:20
  68.5 107.0 %collective-permute-start.5 = (bf16[2,512,384]{2,1,0:T(8,128)(2,1)S(1)}, bf16[2,512,384]{2,1,0:T(8,128)(2,1)}, u32[]{:S(2)}, u32[]{:S(2)}) collective-permute-start(bf16[2,512,384]{2,1,0:T(8,128)(2,1)S(1)} %get-tuple-element.68), channel_id=1, source_target_pairs={{64,0},{72,8},{80,16},{88,24},{96,32},{104,40},{112,48},{120,56},{... | collective-permute-start | bytes 2359304 | tf_op jit(solution)/shard_map/ppermute | solution.py:20
  75.5 101.4 %collective-permute-start.6 = (bf16[2,512,384]{2,1,0:T(8,128)(2,1)S(1)}, bf16[2,512,384]{2,1,0:T(8,128)(2,1)}, u32[]{:S(2)}, u32[]{:S(2)}) collective-permute-start(bf16[2,512,384]{2,1,0:T(8,128)(2,1)S(1)} %get-tuple-element.68), channel_id=1, source_target_pairs={{0,128},{8,136},{16,144},{24,152},{32,160},{40,168},{48,176},{56,1... | collective-permute-start | bytes 2359304 | tf_op jit(solution)/shard_map/ppermute | solution.py:20
  78.6 107.4 %all-to-all-start.2 = ((bf16[16,8,384]{2,0,1:T(8,128)(2,1)}), bf16[16,8,384]{2,0,1:T(8,128)(2,1)}, u32[]{:S(2)}, u32[]{:S(2)}) async-start(bf16[16,8,384]{2,0,1:T(8,128)(2,1)} %bitcast.127), calls=%async_computation.2 | async-start | bytes 196608 | tf_op jit(solution)/shard_map/all_to_all | solution.py:40
  100.5 77.7 %collective-permute-start.7 = (bf16[2,512,384]{2,1,0:T(8,128)(2,1)S(1)}, bf16[2,512,384]{2,1,0:T(8,128)(2,1)S(1)}, u32[]{:S(2)}, u32[]{:S(2)}) collective-permute-start(bf16[2,512,384]{2,1,0:T(8,128)(2,1)S(1)} %get-tuple-element.68), channel_id=1, source_target_pairs={{128,0},{136,8},{144,16},{152,24},{160,32},{168,40},{176,48},{184,... | collective-permute-start | bytes 2359304 | tf_op jit(solution)/shard_map/ppermute | solution.py:20
  166.3 15.4 %collective-permute-start.8 = (bf16[2,512,384]{2,1,0:T(8,128)(2,1)S(1)}, bf16[2,512,384]{2,1,0:T(8,128)(2,1)S(1)}, u32[]{:S(2)}, u32[]{:S(2)}) collective-permute-start(bf16[2,512,384]{2,1,0:T(8,128)(2,1)S(1)} %get-tuple-element.68), channel_id=1, source_target_pairs={{0,256},{8,264},{16,272},{24,280},{32,288},{40,296},{48,304},{56,3... | collective-permute-start | bytes 2359304 | tf_op jit(solution)/shard_map/ppermute | solution.py:20
  167.8 15.6 %collective-permute-start.9 = (bf16[2,512,384]{2,1,0:T(8,128)(2,1)S(1)}, bf16[2,512,384]{2,1,0:T(8,128)(2,1)S(1)}, u32[]{:S(2)}, u32[]{:S(2)}) collective-permute-start(bf16[2,512,384]{2,1,0:T(8,128)(2,1)S(1)} %get-tuple-element.68), channel_id=1, source_target_pairs={{256,0},{264,8},{272,16},{280,24},{288,32},{296,40},{304,48},{312,... | collective-permute-start | bytes 2359304 | tf_op jit(solution)/shard_map/ppermute | solution.py:20
  205.0 15.7 %collective-permute-start.17 = (bf16[2,512,384]{1,2,0:T(8,128)(2,1)S(1)}, bf16[2,512,384]{1,2,0:T(8,128)(2,1)S(1)}, u32[]{:S(2)}, u32[]{:S(2)}) collective-permute-start(bf16[2,512,384]{1,2,0:T(8,128)(2,1)S(1)} %get-tuple-element.40), channel_id=1, source_target_pairs={{0,256},{8,264},{16,272},{24,280},{32,288},{40,296},{48,304},{56,3... | collective-permute-start | bytes 2359304 | tf_op jit(solution)/shard_map/ppermute | solution.py:20
  206.3 22.7 %collective-permute-start.16 = (bf16[2,512,384]{1,2,0:T(8,128)(2,1)S(1)}, bf16[2,512,384]{1,2,0:T(8,128)(2,1)S(1)}, u32[]{:S(2)}, u32[]{:S(2)}) collective-permute-start(bf16[2,512,384]{1,2,0:T(8,128)(2,1)S(1)} %get-tuple-element.41), channel_id=1, source_target_pairs={{256,0},{264,8},{272,16},{280,24},{288,32},{296,40},{304,48},{312,... | collective-permute-start | bytes 2359304 | tf_op jit(solution)/shard_map/ppermute | solution.py:20
  212.5 18.5 %collective-permute-start.15 = (bf16[2,512,384]{1,2,0:T(8,128)(2,1)S(1)}, bf16[2,512,384]{1,2,0:T(8,128)(2,1)S(1)}, u32[]{:S(2)}, u32[]{:S(2)}) collective-permute-start(bf16[2,512,384]{1,2,0:T(8,128)(2,1)S(1)} %get-tuple-element.39), channel_id=1, source_target_pairs={{0,128},{8,136},{16,144},{24,152},{32,160},{40,168},{48,176},{56,1... | collective-permute-start | bytes 2359304 | tf_op jit(solution)/shard_map/ppermute | solution.py:20
  214.4 21.4 %collective-permute-start.14 = (bf16[2,512,384]{1,2,0:T(8,128)(2,1)S(1)}, bf16[2,512,384]{1,2,0:T(8,128)(2,1)S(1)}, u32[]{:S(2)}, u32[]{:S(2)}) collective-permute-start(bf16[2,512,384]{1,2,0:T(8,128)(2,1)S(1)} %get-tuple-element.38), channel_id=1, source_target_pairs={{128,0},{136,8},{144,16},{152,24},{160,32},{168,40},{176,48},{184,... | collective-permute-start | bytes 2359304 | tf_op jit(solution)/shard_map/ppermute | solution.py:20
  218.3 47.5 %collective-permute-start.13 = (bf16[2,512,384]{1,2,0:T(8,128)(2,1)S(1)}, bf16[2,512,384]{1,2,0:T(8,128)(2,1)S(1)}, u32[]{:S(2)}, u32[]{:S(2)}) collective-permute-start(bf16[2,512,384]{1,2,0:T(8,128)(2,1)S(1)} %get-tuple-element.37), channel_id=1, source_target_pairs={{0,64},{8,72},{16,80},{24,88},{32,96},{40,104},{48,112},{56,120},{... | collective-permute-start | bytes 2359304 | tf_op jit(solution)/shard_map/ppermute | solution.py:20
  220.7 62.2 %collective-permute-start.12 = (bf16[2,512,384]{1,2,0:T(8,128)(2,1)S(1)}, bf16[2,512,384]{1,2,0:T(8,128)(2,1)S(1)}, u32[]{:S(2)}, u32[]{:S(2)}) collective-permute-start(bf16[2,512,384]{1,2,0:T(8,128)(2,1)S(1)} %get-tuple-element.36), channel_id=1, source_target_pairs={{64,0},{72,8},{80,16},{88,24},{96,32},{104,40},{112,48},{120,56},{... | collective-permute-start | bytes 2359304 | tf_op jit(solution)/shard_map/ppermute | solution.py:20
  229.0 87.7 %collective-permute-start.11 = (bf16[2,512,384]{1,2,0:T(8,128)(2,1)S(1)}, bf16[2,512,384]{1,2,0:T(8,128)(2,1)S(1)}, u32[]{:S(2)}, u32[]{:S(2)}) collective-permute-start(bf16[2,512,384]{1,2,0:T(8,128)(2,1)S(1)} %get-tuple-element.35), channel_id=1, source_target_pairs={{0,32},{8,40},{16,48},{24,56},{32,64},{40,72},{48,80},{56,88},{64,... | collective-permute-start | bytes 2359304 | tf_op jit(solution)/shard_map/ppermute | solution.py:20
  231.0 90.0 %collective-permute-start.10 = (bf16[2,512,384]{1,2,0:T(8,128)(2,1)S(1)}, bf16[2,512,384]{1,2,0:T(8,128)(2,1)S(1)}, u32[]{:S(2)}, u32[]{:S(2)}) collective-permute-start(bf16[2,512,384]{1,2,0:T(8,128)(2,1)S(1)} %get-tuple-element.34), channel_id=1, source_target_pairs={{32,0},{40,8},{48,16},{56,24},{64,32},{72,40},{80,48},{88,56},{96,... | collective-permute-start | bytes 2359304 | tf_op jit(solution)/shard_map/ppermute | solution.py:20
  322.0 21.6 %collective-permute-start.18 = (f32[2,256,384]{1,2,0:T(8,128)S(1)}, f32[2,256,384]{1,2,0:T(8,128)}, u32[]{:S(2)}, u32[]{:S(2)}) collective-permute-start(f32[2,256,384]{1,2,0:T(8,128)S(1)} %slice_select_fusion), channel_id=1, source_target_pairs={{0,16},{8,24},{16,0},{24,8},{32,48},{40,56},{48,32},{56,40},{64,80... | collective-permute-start | bytes 2359304 | tf_op jit(solution)/shard_map/ppermute | solution.py:14
  328.0 21.5 %all-to-all-start.3 = ((bf16[8,16,384]{2,1,0:T(8,128)(2,1)}), bf16[8,16,384]{2,1,0:T(8,128)(2,1)}, u32[]{:S(2)}, u32[]{:S(2)}) async-start(bf16[8,16,384]{2,1,0:T(8,128)(2,1)} %bitcast.149), calls=%async_computation.3 | async-start | bytes 196608 | tf_op jit(solution)/shard_map/all_to_all | solution.py:164
  349.5 16.2 %all-to-all-start.5 = ((bf16[8,16,384]{2,1,0:T(8,128)(2,1)}), bf16[8,16,384]{2,1,0:T(8,128)(2,1)S(1)}, u32[]{:S(2)}, u32[]{:S(2)}) async-start(bf16[8,16,384]{2,1,0:T(8,128)(2,1)} %bitcast.24), calls=%async_computation.5 | async-start | bytes 196608 | tf_op jit(solution)/shard_map/all_to_all | solution.py:165
  365.7 12.0 %all-to-all-start.6 = ((bf16[8,16,384]{2,1,0:T(8,128)(2,1)}), bf16[8,16,384]{2,1,0:T(8,128)(2,1)S(1)}, u32[]{:S(2)}, u32[]{:S(2)}) async-start(bf16[8,16,384]{2,1,0:T(8,128)(2,1)} %bitcast.28), calls=%async_computation.6 | async-start | bytes 196608 | tf_op jit(solution)/shard_map/all_to_all | solution.py:166
  (19 other events, 202.7 us)
where the time goes:
time: 393 us; the launch traced here: 390 us
  waiting for transfers between devices  215 us (55%)
  starting transfers between devices  118 us (30%)
  local copies, waits for them, and re-layouts  24.6 us (6%)
  matrix products  20.7 us (5%)
  other arithmetic  10.4 us (3%)
    ppermute x16, waiting for transfers between devices, passed_along(): return lax.ppermute(shard, axis, pairs)  166 us
    ppermute x16, starting transfers between devices, passed_along(): return lax.ppermute(shard, axis, pairs)  62.1 us
    ppermute x4, waiting for transfers between devices, partner_2(): lax.ppermute(shard, axis, [(i, i ^ 1 << distance) for i in range(lax.axis...  12.8 us
    ppermute x4, starting transfers between devices, partner_2(): lax.ppermute(shard, axis, [(i, i ^ 1 << distance) for i in range(lax.axis...  11 us
    all_to_all x1, starting transfers between devices, per_device(): lax.all_to_all(value_rows, 'head', split_axis=1, concat_axis=0, tiled=True)  10.3 us
    all_to_all x1, waiting for transfers between devices, per_device(): lax.all_to_all(grad_query, 'head', split_axis=0, concat_axis=1, tiled=True)  8.26 us
    unnamed x47, local copies, waits for them, and re-layouts  8.07 us
    all_to_all x1, waiting for transfers between devices, per_device(): lax.all_to_all(grad_keys, 'head', split_axis=0, concat_axis=1, tiled=True)  7.89 us
  transfers between devices with their start and end apart: 28, of which 17 were waited for; matrix products, arithmetic and copies ran while one was open for 9% of the time, Pallas kernels for 0%

commit v1 on v0

v1 whole, which is shorter than its diff:
```python
import math

import jax
import jax.numpy as jnp
from jax import lax
from jax.experimental import pallas as pl
from jax.experimental.pallas import tpu as pltpu
from jax.sharding import PartitionSpec as P

HD = 128
HEADS = 24
FT = 512
FRAMES = 16
SUB = 16
OWNERS = 32
PLANES = 8
PER_PLANE = 3
UNITS = 8
SCALE = 1.0 / math.sqrt(HD)
EXP2 = SCALE * math.log2(math.e)
BF = jnp.bfloat16
F32 = jnp.float32


def place(head, frame):
    plane = head // PER_PLANE
    pair = (head % PER_PLANE + plane) % 4
    col = frame % 4
    seq = ((frame // 4) * 8 + 2 * pair + col % 2) * 2 + col // 2
    return seq, plane


def shift_of(rel):
    return (1 - 2 * (rel % 2)) * lax.shift_left(jnp.int32(1), rel // 2)


def inside(frame):
    return (frame >= 0) & (frame < FRAMES)


def sent_to(frame, rel):
    there = jnp.where(rel == 6, (frame + 8) % FRAMES, frame + shift_of(rel))
    return there, inside(there)


def came_from(frame, rel):
    there = jnp.where(rel == 6, (frame + 8) % FRAMES, frame - shift_of(rel))
    return there, inside(there)


def attention_kernel(
    q_in, k_in, v_in, g_in, mask,
    o_out, dq_out, dk_out, dv_out,
    rows, kv, qg, scores, gradw, weights, scores_b, parts, back, outs,
    peak, acc, dq_acc, rowl, rowd, qt, gt, bias,
    in_sem, s1, r1, s2, r2, s3, r3, s4, r4,
):
    seq = lax.axis_index("seq")
    plane = lax.axis_index("head")
    src_frame = seq // 4
    src_spot = (seq % 4) * 8 + plane
    a = seq // 16
    y = (seq // 2) % 8
    col = (seq % 2) * 2 + y % 2
    frame = 4 * a + col
    within = (y // 2 + 8 - plane) % 4
    busy = within < PER_PLANE
    head = plane * PER_PLANE + within
    own_hit = busy & (frame == src_frame)

    def is_me(target):
        return (target[0] == seq) & (target[1] == plane)

    def owner(spot):
        return frame * 4 + spot // 8, spot % 8

    fetch = [
        pltpu.make_async_copy(ref, rows.at[n], in_sem.at[n])
        for n, ref in enumerate((k_in, v_in, q_in, g_in))
    ]
    for copy in fetch:
        copy.start()

    barrier = pltpu.get_barrier_semaphore()

    def greet(target):
        @pl.when(jnp.logical_not(is_me(target)))
        def _():
            pl.semaphore_signal(
                barrier, inc=1, device_id=target, device_id_type=pl.DeviceIdType.MESH
            )

    def greet_head(n, carry):
        greet(place(n, src_frame))
        return carry

    lax.fori_loop(0, HEADS, greet_head, 0)

    @pl.when(busy)
    def _():
        def greet_owner(n, carry):
            greet(owner(n))
            return carry

        lax.fori_loop(0, OWNERS, greet_owner, 0)

        def greet_partner(rel, carry):
            there, ok = sent_to(frame, rel)

            @pl.when(ok)
            def _():
                greet(place(head, there))

            return carry

        lax.fori_loop(0, UNITS - 1, greet_partner, 0)

    partners = jnp.int32(0)
    for rel in range(UNITS - 1):
        partners = partners + came_from(frame, jnp.int32(rel))[1].astype(jnp.int32)
    hit = own_hit.astype(jnp.int32)
    expected = HEADS - hit + busy.astype(jnp.int32) * (OWNERS - hit + partners)
    for copy in fetch:
        copy.wait()
    pl.semaphore_wait(barrier, expected)

    def scatter(stage, dst):
        def piece(n):
            k = n // PER_PLANE
            off = (4 + ((k + 1) // 2) * (2 * (k % 2) - 1) + 8) % 8
            to_head = ((plane + off) % PLANES) * PER_PLANE + n % PER_PLANE
            target = place(to_head, src_frame)
            src = rows.at[
                pl.ds(2 * stage, 2), :, pl.ds(pl.multiple_of(to_head * HD, HD), HD)
            ]
            to = dst.at[:, pl.ds(pl.multiple_of(src_spot * SUB, SUB), SUB), :]
            return target, src, to

        def remote(target, src, to):
            return pltpu.make_async_remote_copy(
                src_ref=src, dst_ref=to, send_sem=s1.at[stage], recv_sem=r1.at[stage],
                device_id=target, device_id_type=pl.DeviceIdType.MESH,
            )

        def send(n, carry):
            target, src, to = piece(n)
            mine = is_me(target)

            @pl.when(mine)
            def _():
                pltpu.make_async_copy(src, to, r1.at[stage]).start()

            @pl.when(jnp.logical_not(mine))
            def _():
                remote(target, src, to).start()

            return carry

        def sent(n, carry):
            target, src, to = piece(n)

            @pl.when(jnp.logical_not(is_me(target)))
            def _():
                remote(target, src, to).wait_send()

            return carry

        return send, sent

    send_kv, sent_kv = scatter(0, kv.at[0])
    send_qg, sent_qg = scatter(1, qg)
    lax.fori_loop(0, HEADS, send_kv, 0)
    lax.fori_loop(0, HEADS, send_qg, 0)

    def kv_copy(rel):
        there, ok = sent_to(frame, rel)
        copy = pltpu.make_async_remote_copy(
            src_ref=kv.at[0], dst_ref=kv.at[rel + 1], send_sem=s2.at[rel], recv_sem=r2.at[rel],
            device_id=place(head, there), device_id_type=pl.DeviceIdType.MESH,
        )
        return copy, ok

    def grad_copy(rel):
        there, ok = came_from(frame, rel)
        copy = pltpu.make_async_remote_copy(
            src_ref=parts.at[rel + 1], dst_ref=back.at[rel], send_sem=s3.at[rel],
            recv_sem=r3.at[rel],
            device_id=place(head, there), device_id_type=pl.DeviceIdType.MESH,
        )
        return copy, ok

    def result_copy(array, spot):
        target = owner(spot)
        src = outs.at[array, pl.ds(pl.multiple_of(spot * SUB, SUB), SUB), :]
        dst = (o_out, dq_out, dk_out, dv_out)[array].at[
            :, pl.ds(pl.multiple_of(head * HD, HD), HD)
        ]
        remote = pltpu.make_async_remote_copy(
            src_ref=src, dst_ref=dst, send_sem=s4.at[array], recv_sem=r4.at[array],
            device_id=target, device_id_type=pl.DeviceIdType.MESH,
        )
        return is_me(target), remote, pltpu.make_async_copy(src, dst, r4.at[array])

    def give_result(array):
        def send(spot, carry):
            mine, remote, local = result_copy(array, spot)

            @pl.when(mine)
            def _():
                local.start()

            @pl.when(jnp.logical_not(mine))
            def _():
                remote.start()

            return carry

        lax.fori_loop(0, OWNERS, send, 0)

    @pl.when(busy)
    def _():
        pltpu.make_async_copy(kv.at[0], kv.at[0], r1.at[0]).wait()

        def send_partner(rel, carry):
            copy, ok = kv_copy(rel)

            @pl.when(ok)
            def _():
                copy.start()

            return carry

        lax.fori_loop(0, UNITS - 1, send_partner, 0)

        lane_block = lax.broadcasted_iota(jnp.int32, (8, FT), 1) // 128
        bias[16] = jnp.zeros((8, FT), F32)

        def bias_row(n, carry):
            row = jnp.zeros((8, FT), F32)
            for kb in range(4):
                seen = mask[n // 4, n % 4, kb] > 0
                row = jnp.where(
                    (lane_block == kb) & jnp.logical_not(seen), jnp.float32(-jnp.inf), row
                )
            bias[n] = row
            return carry

        lax.fori_loop(0, 16, bias_row, 0)
        peak[...] = jnp.full((FT, HD), -jnp.inf, F32)
        acc[...] = jnp.zeros((FT, HD), F32)
        dq_acc[...] = jnp.zeros((FT, HD), F32)
        rowl[...] = jnp.zeros((FT, HD), F32)

        pltpu.make_async_copy(qg, qg, r1.at[1]).wait()
        qt[...] = qg[0].T

        def has_unit(u):
            return (u == 0) | came_from(frame, u - 1 + (u == 0).astype(jnp.int32))[1]

        def first_pass(u, carry):
            @pl.when(has_unit(u))
            def _():
                @pl.when(u > 0)
                def _():
                    pltpu.make_async_copy(kv.at[u], kv.at[u], r2.at[u - 1]).wait()

                keys = kv[u, 0]
                values = kv[u, 1]
                for qb in range(4):
                    band = pl.ds(qb * 128, 128)
                    which = jnp.where(u == 0, 16, ((u + 1) // 2 - 1) * 4 + qb)
                    s = lax.dot_general(
                        qg[0, band], keys, (((1,), (1,)), ((), ())), preferred_element_type=F32
                    )
                    s = s + bias[which, 0:1, :]
                    scores[u, band] = s
                    top = jnp.maximum(
                        jnp.maximum(s[:, 0:128], s[:, 128:256]),
                        jnp.maximum(s[:, 256:384], s[:, 384:512]),
                    )
                    peak[band] = jnp.maximum(peak[band], top)
                    gradw[u, band] = lax.dot_general(
                        qg[1, band], values, (((1,), (1,)), ((), ())), preferred_element_type=F32
                    )

            return carry

        lax.fori_loop(0, UNITS, first_pass, 0)
        top = jnp.max(peak[...], axis=1, keepdims=True) * EXP2
        peak[...] = jnp.broadcast_to(top, (FT, HD))

        def second_pass(u, carry):
            @pl.when(has_unit(u))
            def _():
                for qb in range(4):
                    band = pl.ds(qb * 128, 128)
                    e = jnp.exp2(scores[u, band] * EXP2 - peak[band, 0:1])
                    rowl[band] += (e[:, 0:128] + e[:, 128:256]) + (e[:, 256:384] + e[:, 384:512])
                    weights[u, band] = e.astype(BF)
                acc[...] += jnp.dot(weights[u], kv[u, 1], preferred_element_type=F32)

            return carry

        lax.fori_loop(0, UNITS, second_pass, 0)
        inv = 1.0 / jnp.sum(rowl[...], axis=1, keepdims=True)
        attended = (acc[...] * inv).astype(BF)
        outs[0] = attended
        give_result(0)
        grads = qg[1].astype(F32)
        delta = jnp.sum(grads * attended.astype(F32), axis=1, keepdims=True)
        gt[...] = (grads * inv).astype(BF).T
        inv = inv * SCALE
        rowl[...] = jnp.broadcast_to(inv, (FT, HD))
        rowd[...] = jnp.broadcast_to(inv * delta, (FT, HD))

        def third_pass(n, carry):
            u = UNITS - 1 - n

            @pl.when(has_unit(u))
            def _():
                for qb in range(4):
                    band = pl.ds(qb * 128, 128)
                    ds = weights[u, band].astype(F32) * (
                        gradw[u, band] * rowl[band, 0:1] - rowd[band, 0:1]
                    )
                    scores_b[u, band] = ds.astype(BF)
                ds = scores_b[u]
                parts[u, 0] = jnp.dot(qt[...], ds, preferred_element_type=F32).astype(BF)
                parts[u, 1] = jnp.dot(gt[...], weights[u], preferred_element_type=F32).astype(BF)

                @pl.when(u > 0)
                def _():
                    grad_copy(u - 1)[0].start()

                dq_acc[...] += jnp.dot(ds, kv[u, 0], preferred_element_type=F32)

            return carry

        lax.fori_loop(0, UNITS, third_pass, 0)
        outs[1] = dq_acc[...].astype(BF)
        give_result(1)

        sums = scores.at[0, pl.ds(0, 256)]
        sums[0:128] = parts[0, 0].astype(F32)
        sums[128:256] = parts[0, 1].astype(F32)

        def add_back(rel, carry):
            @pl.when(sent_to(frame, rel)[1])
            def _():
                pltpu.make_async_copy(back.at[rel], back.at[rel], r3.at[rel]).wait()
                sums[0:128] += back[rel, 0].astype(F32)
                sums[128:256] += back[rel, 1].astype(F32)

            return carry

        lax.fori_loop(0, UNITS - 1, add_back, 0)
        outs[2] = sums[0:128].T.astype(BF)
        give_result(2)
        outs[3] = sums[128:256].T.astype(BF)
        give_result(3)

        def partner_sent(rel, carry):
            copy, ok = kv_copy(rel)

            @pl.when(ok)
            def _():
                copy.wait_send()

            copy, ok = grad_copy(rel)

            @pl.when(ok)
            def _():
                copy.wait_send()

            return carry

        lax.fori_loop(0, UNITS - 1, partner_sent, 0)
        for array in range(4):

            def result_sent(spot, carry, array=array):
                mine, remote, _ = result_copy(array, spot)

                @pl.when(jnp.logical_not(mine))
                def _():
                    remote.wait_send()

                return carry

            lax.fori_loop(0, OWNERS, result_sent, 0)

    lax.fori_loop(0, HEADS, sent_kv, 0)
    lax.fori_loop(0, HEADS, sent_qg, 0)
    for n, ref in enumerate((o_out, dq_out, dk_out, dv_out)):
        pltpu.make_async_copy(ref, ref, r4.at[n]).wait()


def per_device(query_rows, key_rows, value_rows, out_grad, block_mask):
    anywhere = pl.BlockSpec(memory_space=pl.ANY)
    result = jax.ShapeDtypeStruct(query_rows.shape, BF)
    dma = pltpu.SemaphoreType.DMA
    return pl.pallas_call(
        attention_kernel,
        out_shape=(result,) * 4,
        in_specs=[anywhere] * 4 + [pl.BlockSpec(memory_space=pltpu.SMEM)],
        out_specs=(anywhere,) * 4,
        scratch_shapes=[
            pltpu.VMEM((4, SUB, HEADS * HD), BF),
            pltpu.VMEM((UNITS, 2, FT, HD), BF),
            pltpu.VMEM((2, FT, HD), BF),
            pltpu.VMEM((UNITS, FT, FT), F32),
            pltpu.VMEM((UNITS, FT, FT), F32),
            pltpu.VMEM((UNITS, FT, FT), BF),
            pltpu.VMEM((UNITS, FT, FT), BF),
            pltpu.VMEM((UNITS, 2, HD, FT), BF),
            pltpu.VMEM((UNITS - 1, 2, HD, FT), BF),
            pltpu.VMEM((4, FT, HD), BF),
            pltpu.VMEM((FT, HD), F32),
            pltpu.VMEM((FT, HD), F32),
            pltpu.VMEM((FT, HD), F32),
            pltpu.VMEM((FT, HD), F32),
            pltpu.VMEM((FT, HD), F32),
            pltpu.VMEM((HD, FT), BF),
            pltpu.VMEM((HD, FT), BF),
            pltpu.VMEM((17, 8, FT), F32),
            dma((4,)),
            dma((2,)),
            dma((2,)),
            dma((UNITS - 1,)),
            dma((UNITS - 1,)),
            dma((UNITS - 1,)),
            dma((UNITS - 1,)),
            dma((4,)),
            dma((4,)),
        ],
        compiler_params=pltpu.CompilerParams(
            collective_id=0, has_side_effects=True, vmem_limit_bytes=48 * 1024 * 1024
        ),
    )(query_rows, key_rows, value_rows, out_grad, block_mask)


def solution(mesh):
    tokens = P(("seq", "head"), None)
    return jax.shard_map(
        per_device,
        mesh=mesh,
        in_specs=(tokens,) * 4 + (P(),),
        out_specs=(tokens,) * 4,
        check_vma=False,
    )
```

time: 393 us -> 89.6 us (0.23)
  the two profiles are of different devices: /device:TPU:20 before, /device:TPU:11 now
where the time goes in v1:
time: 89.6 us; the launch traced here: 89.4 us
  Pallas kernels  81.9 us (91%)
  local copies, waits for them, and re-layouts  6.82 us (8%)
    pallas_call x1, Pallas kernels, per_device(): pl.pallas_call(attention_kernel, out_shape=(result,) * 4, in_specs=[anywh...  81.9 us
    unnamed x14, local copies, waits for them, and re-layouts  6.82 us

profile of v1, /device:TPU:11, one launch (start us, length us, event | category | flops | bytes accessed | tf_op | source)
XLA Modules:
  0.0 89.4 jit_solution(4301072029802118665)
XLA Ops:
  0.6 0.0 copy-start
  0.6 0.9 copy-done
  1.5 0.0 copy-start.1
  1.5 0.9 copy-done.1
  2.4 0.0 copy-start.2
  2.4 0.9 copy-done.2
  3.3 0.0 copy-start.3
  3.3 0.9 copy-done.3
  4.2 0.0 copy-start.4
  4.2 0.7 copy-done.4
  4.9 81.9 %shard_map.84 = (bf16[16,3072]{1,0:T(8,128)(2,1)S(1)}, bf16[16,3072]{1,0:T(8,128)(2,1)S(1)}, bf16[16,3072]{1,0:T(8,128)(2,1)S(1)}, bf16[16,3072]{1,0:T(8,128)(2,1)S(1)}) custom-call(bf16[16,3072]{1,0:T(8,128)(2,1)S(1)} %copy-done, bf16[16,3072]{1,0:T(8,128)(2,1)S(1)} %copy-done.1, bf16[16,3072]{1,0:T(8,128)(2,1)S(1)} %copy-done.2, ...), custom_call_target="tpu_custom_call" | custom-call | tf_op jit(solution)/shard_map/pallas_call | solution.py:401
  86.8 0.6 copy.13
  87.4 0.6 copy.14
  88.1 0.6 copy.15
  88.7 0.6 copy.16
Async XLA Ops:
  0.6 0.9 %copy-start = (bf16[16,3072]{1,0:T(8,128)(2,1)S(1)}, bf16[16,3072]{1,0:T(8,128)(2,1)}, u32[]{:S(2)}) copy-start(bf16[16,3072]{1,0:T(8,128)(2,1)} %q_in.1) | copy-start | bytes 294916
  1.5 0.9 copy-start.1
  2.4 0.9 copy-start.2
  3.3 0.9 copy-start.3
  4.2 0.7 copy-start.4

commit v2 on v1

--- a/solution.py
+++ b/solution.py
@@ -20,18 +20,15 @@
 EXP2 = SCALE * math.log2(math.e)
 BF = jnp.bfloat16
 F32 = jnp.float32
-
-
-def place(head, frame):
-    plane = head // PER_PLANE
-    pair = (head % PER_PLANE + plane) % 4
-    col = frame % 4
-    seq = ((frame // 4) * 8 + 2 * pair + col % 2) * 2 + col // 2
-    return seq, plane
+VMEM_MB = 60
+
+
+def seat(pair, frame):
+    return (frame >> 2) * 16 + pair * 4 + (frame & 1) * 2 + ((frame >> 1) & 1)
 
 
 def shift_of(rel):
-    return (1 - 2 * (rel % 2)) * lax.shift_left(jnp.int32(1), rel // 2)
+    return (1 - 2 * (rel & 1)) * lax.shift_left(jnp.int32(1), rel >> 1)
 
 
 def inside(frame):
@@ -39,12 +36,12 @@
 
 
 def sent_to(frame, rel):
-    there = jnp.where(rel == 6, (frame + 8) % FRAMES, frame + shift_of(rel))
+    there = jnp.where(rel == 6, (frame + 8) & 15, frame + shift_of(rel))
     return there, inside(there)
 
 
 def came_from(frame, rel):
-    there = jnp.where(rel == 6, (frame + 8) % FRAMES, frame - shift_of(rel))
+    there = jnp.where(rel == 6, (frame + 8) & 15, frame - shift_of(rel))
     return there, inside(there)
 
 
@@ -57,22 +54,17 @@
 ):
     seq = lax.axis_index("seq")
     plane = lax.axis_index("head")
-    src_frame = seq // 4
-    src_spot = (seq % 4) * 8 + plane
-    a = seq // 16
-    y = (seq // 2) % 8
-    col = (seq % 2) * 2 + y % 2
-    frame = 4 * a + col
-    within = (y // 2 + 8 - plane) % 4
+    src_frame = seq >> 2
+    src_spot = (seq & 3) * 8 + plane
+    frame = (seq >> 4) * 4 + (seq & 1) * 2 + ((seq >> 1) & 1)
+    pair = (seq >> 2) & 3
+    within = (pair - plane) & 3
     busy = within < PER_PLANE
     head = plane * PER_PLANE + within
     own_hit = busy & (frame == src_frame)
-
-    def is_me(target):
-        return (target[0] == seq) & (target[1] == plane)
-
-    def owner(spot):
-        return frame * 4 + spot // 8, spot % 8
+    my_head = jnp.where(own_hit, head, -1)
+    my_spot = jnp.where(own_hit, src_spot, -1)
+    seat0 = seat(0, src_frame)
 
     fetch = [
         pltpu.make_async_copy(ref, rows.at[n], in_sem.at[n])
@@ -84,32 +76,26 @@
     barrier = pltpu.get_barrier_semaphore()
 
     def greet(target):
-        @pl.when(jnp.logical_not(is_me(target)))
-        def _():
-            pl.semaphore_signal(
-                barrier, inc=1, device_id=target, device_id_type=pl.DeviceIdType.MESH
-            )
-
-    def greet_head(n, carry):
-        greet(place(n, src_frame))
-        return carry
-
-    lax.fori_loop(0, HEADS, greet_head, 0)
+        pl.semaphore_signal(
+            barrier, inc=1, device_id=target, device_id_type=pl.DeviceIdType.MESH
+        )
 
     @pl.when(busy)
     def _():
-        def greet_owner(n, carry):
-            greet(owner(n))
-            return carry
-
-        lax.fori_loop(0, OWNERS, greet_owner, 0)
+        def greet_owners(z, carry):
+            for r in range(4):
+                greet((frame * 4 + r, z))
+
+            return carry
+
+        lax.fori_loop(0, PLANES, greet_owners, 0)
 
         def greet_partner(rel, carry):
             there, ok = sent_to(frame, rel)
 
             @pl.when(ok)
             def _():
-                greet(place(head, there))
+                greet((seat(pair, there), plane))
 
             return carry
 
@@ -118,65 +104,51 @@
     partners = jnp.int32(0)
     for rel in range(UNITS - 1):
         partners = partners + came_from(frame, jnp.int32(rel))[1].astype(jnp.int32)
-    hit = own_hit.astype(jnp.int32)
-    expected = HEADS - hit + busy.astype(jnp.int32) * (OWNERS - hit + partners)
+    expected = HEADS + busy.astype(jnp.int32) * partners
     for copy in fetch:
         copy.wait()
     pl.semaphore_wait(barrier, expected)
 
     def scatter(stage, dst):
-        def piece(n):
-            k = n // PER_PLANE
-            off = (4 + ((k + 1) // 2) * (2 * (k % 2) - 1) + 8) % 8
-            to_head = ((plane + off) % PLANES) * PER_PLANE + n % PER_PLANE
-            target = place(to_head, src_frame)
-            src = rows.at[
-                pl.ds(2 * stage, 2), :, pl.ds(pl.multiple_of(to_head * HD, HD), HD)
-            ]
-            to = dst.at[:, pl.ds(pl.multiple_of(src_spot * SUB, SUB), SUB), :]
-            return target, src, to
-
-        def remote(target, src, to):
-            return pltpu.make_async_remote_copy(
-                src_ref=src, dst_ref=to, send_sem=s1.at[stage], recv_sem=r1.at[stage],
-                device_id=target, device_id_type=pl.DeviceIdType.MESH,
-            )
-
-        def send(n, carry):
-            target, src, to = piece(n)
-            mine = is_me(target)
-
-            @pl.when(mine)
-            def _():
-                pltpu.make_async_copy(src, to, r1.at[stage]).start()
-
-            @pl.when(jnp.logical_not(mine))
-            def _():
-                remote(target, src, to).start()
-
-            return carry
-
-        def sent(n, carry):
-            target, src, to = piece(n)
-
-            @pl.when(jnp.logical_not(is_me(target)))
-            def _():
-                remote(target, src, to).wait_send()
-
-            return carry
-
-        return send, sent
-
-    send_kv, sent_kv = scatter(0, kv.at[0])
-    send_qg, sent_qg = scatter(1, qg)
-    lax.fori_loop(0, HEADS, send_kv, 0)
-    lax.fori_loop(0, HEADS, send_qg, 0)
+        to = dst.at[:, pl.ds(pl.multiple_of(src_spot * SUB, SUB), SUB), :]
+
+        def send(k, carry):
+            off = 4 + ((k + 1) >> 1) * (2 * (k & 1) - 1)
+            z = (plane + off) & 7
+            for c in range(PER_PLANE):
+                to_head = z * PER_PLANE + c
+                src = rows.at[
+                    pl.ds(2 * stage, 2), :, pl.ds(pl.multiple_of(to_head * HD, HD), HD)
+                ]
+                mine = to_head == my_head
+
+                @pl.when(mine)
+                def _(src=src):
+                    pltpu.make_async_copy(src, to, r1.at[stage]).start()
+
+                @pl.when(jnp.logical_not(mine))
+                def _(src=src, c=c):
+                    pltpu.make_async_remote_copy(
+                        src_ref=src, dst_ref=to, send_sem=s1.at[stage], recv_sem=r1.at[stage],
+                        device_id=(seat0 + ((c + z) & 3) * 4, z),
+                        device_id_type=pl.DeviceIdType.MESH,
+                    ).start()
+
+            return carry
+
+        lax.fori_loop(0, PLANES, send, 0)
+
+    def wait_for(ref, sem):
+        pltpu.make_async_copy(ref, ref, sem).wait()
+
+    scatter(0, kv.at[0])
+    scatter(1, qg)
 
     def kv_copy(rel):
         there, ok = sent_to(frame, rel)
         copy = pltpu.make_async_remote_copy(
             src_ref=kv.at[0], dst_ref=kv.at[rel + 1], send_sem=s2.at[rel], recv_sem=r2.at[rel],
-            device_id=place(head, there), device_id_type=pl.DeviceIdType.MESH,
+            device_id=(seat(pair, there), plane), device_id_type=pl.DeviceIdType.MESH,
         )
         return copy, ok
 
@@ -185,37 +157,35 @@
         copy = pltpu.make_async_remote_copy(
             src_ref=parts.at[rel + 1], dst_ref=back.at[rel], send_sem=s3.at[rel],
             recv_sem=r3.at[rel],
-            device_id=place(head, there), device_id_type=pl.DeviceIdType.MESH,
+            device_id=(seat(pair, there), plane), device_id_type=pl.DeviceIdType.MESH,
         )
         return copy, ok
 
-    def result_copy(array, spot):
-        target = owner(spot)
-        src = outs.at[array, pl.ds(pl.multiple_of(spot * SUB, SUB), SUB), :]
+    def give_result(array):
         dst = (o_out, dq_out, dk_out, dv_out)[array].at[
             :, pl.ds(pl.multiple_of(head * HD, HD), HD)
         ]
-        remote = pltpu.make_async_remote_copy(
-            src_ref=src, dst_ref=dst, send_sem=s4.at[array], recv_sem=r4.at[array],
-            device_id=target, device_id_type=pl.DeviceIdType.MESH,
-        )
-        return is_me(target), remote, pltpu.make_async_copy(src, dst, r4.at[array])
-
-    def give_result(array):
-        def send(spot, carry):
-            mine, remote, local = result_copy(array, spot)
-
-            @pl.when(mine)
-            def _():
-                local.start()
-
-            @pl.when(jnp.logical_not(mine))
-            def _():
-                remote.start()
-
-            return carry
-
-        lax.fori_loop(0, OWNERS, send, 0)
+
+        def send(z, carry):
+            for r in range(4):
+                spot = r * 8 + z
+                src = outs.at[array, pl.ds(pl.multiple_of(spot * SUB, SUB), SUB), :]
+                mine = spot == my_spot
+
+                @pl.when(mine)
+                def _(src=src):
+                    pltpu.make_async_copy(src, dst, r4.at[array]).start()
+
+                @pl.when(jnp.logical_not(mine))
+                def _(src=src, r=r):
+                    pltpu.make_async_remote_copy(
+                        src_ref=src, dst_ref=dst, send_sem=s4.at[array], recv_sem=r4.at[array],
+                        device_id=(frame * 4 + r, z), device_id_type=pl.DeviceIdType.MESH,
+                    ).start()
+
+            return carry
+
+        lax.fori_loop(0, PLANES, send, 0)
 
     @pl.when(busy)
     def _():
@@ -377,19 +347,25 @@
         lax.fori_loop(0, UNITS - 1, partner_sent, 0)
         for array in range(4):
 
-            def result_sent(spot, carry, array=array):
-                mine, remote, _ = result_copy(array, spot)
-
-                @pl.when(jnp.logical_not(mine))
-                def _():
-                    remote.wait_send()
-
-                return carry
-
-            lax.fori_loop(0, OWNERS, result_sent, 0)
-
-    lax.fori_loop(0, HEADS, sent_kv, 0)
-    lax.fori_loop(0, HEADS, sent_qg, 0)
+            @pl.when(own_hit)
+            def _(array=array):
+                wait_for(outs.at[array, pl.ds(0, FT - SUB)], s4.at[array])
+
+            @pl.when(jnp.logical_not(own_hit))
+            def _(array=array):
+                wait_for(outs.at[array], s4.at[array])
+
+    for stage in range(2):
+        sent = rows.at[pl.ds(2 * stage, 2)]
+
+        @pl.when(own_hit)
+        def _(sent=sent, stage=stage):
+            wait_for(sent.at[:, :, pl.ds(0, (HEADS - 1) * HD)], s1.at[stage])
+
+        @pl.when(jnp.logical_not(own_hit))
+        def _(sent=sent, stage=stage):
+            wait_for(sent, s1.at[stage])
+
     for n, ref in enumerate((o_out, dq_out, dk_out, dv_out)):
         pltpu.make_async_copy(ref, ref, r4.at[n]).wait()
 
@@ -433,7 +409,7 @@
             dma((4,)),
         ],
         compiler_params=pltpu.CompilerParams(
-            collective_id=0, has_side_effects=True, vmem_limit_bytes=48 * 1024 * 1024
+            collective_id=0, has_side_effects=True, vmem_limit_bytes=VMEM_MB * 1024 * 1024
         ),
     )(query_rows, key_rows, value_rows, out_grad, block_mask)
 

time: 89.6 us -> 82.4 us (0.920)
  the two profiles are of different devices: /device:TPU:11 before, /device:TPU:3 now
where the time goes in v2:
time: 82.4 us; the launch traced here: 82.1 us
  Pallas kernels  77.4 us (94%)
  local copies, waits for them, and re-layouts  4.07 us (5%)
    pallas_call x1, Pallas kernels, per_device(): pl.pallas_call(attention_kernel, out_shape=(result,) * 4, in_specs=[anywh...  77.4 us
    unnamed x10, local copies, waits for them, and re-layouts  4.07 us

profile of v2, /device:TPU:3, one launch (start us, length us, event | category | flops | bytes accessed | tf_op | source)
XLA Modules:
  0.0 82.1 jit_solution(10515269356135138578)
XLA Ops:
  0.6 77.4 %shard_map.84 = (bf16[16,3072]{1,0:T(8,128)(2,1)}, bf16[16,3072]{1,0:T(8,128)(2,1)}, bf16[16,3072]{1,0:T(8,128)(2,1)}, bf16[16,3072]{1,0:T(8,128)(2,1)}) custom-call(bf16[16,3072]{1,0:T(8,128)(2,1)} %q_in.1, bf16[16,3072]{1,0:T(8,128)(2,1)} %k_in.1, bf16[16,3072]{1,0:T(8,128)(2,1)} %v_in.1, bf16[16,3072]{1,0:T(8,128)(2,1)} %g_in.1, s32[4,4,4]{2,1,0:T(4,128)} %mask.1), custom_call_target="tpu_custom_call" | custom-call | tf_op jit(solution)/shard_map/pallas_call | solution.py:377
  78.0 0.0 copy-start.2
  78.0 1.6 %copy.13 = bf16[16,3072]{1,0:T(8,128)(2,1)} copy(bf16[16,3072]{1,0:T(8,128)(2,1)} %get-tuple-element.8) | data formatting | bytes 196608
  79.6 0.0 copy-done.2
  79.6 0.0 copy-start.1
  79.6 0.6 copy.14
  80.3 0.3 copy-done.1
  80.5 0.0 copy-start
  80.6 0.6 copy.15
  81.2 0.3 copy-done
  81.5 0.6 copy.16
Async XLA Ops:
  78.0 1.6 %copy-start.2 = (bf16[16,3072]{1,0:T(8,128)(2,1)S(1)}, bf16[16,3072]{1,0:T(8,128)(2,1)}, u32[]{:S(2)}) copy-start(bf16[16,3072]{1,0:T(8,128)(2,1)} %get-tuple-element.9) | copy-start | bytes 294916
  79.6 0.9 %copy-start.1 = (bf16[16,3072]{1,0:T(8,128)(2,1)S(1)}, bf16[16,3072]{1,0:T(8,128)(2,1)}, u32[]{:S(2)}) copy-start(bf16[16,3072]{1,0:T(8,128)(2,1)} %get-tuple-element.10) | copy-start | bytes 294916
  80.5 0.9 %copy-start = (bf16[16,3072]{1,0:T(8,128)(2,1)S(1)}, bf16[16,3072]{1,0:T(8,128)(2,1)}, u32[]{:S(2)}) copy-start(bf16[16,3072]{1,0:T(8,128)(2,1)} %get-tuple-element.11) | copy-start | bytes 294916

commit v3 on v2

--- a/solution.py
+++ b/solution.py
@@ -21,6 +21,7 @@
 BF = jnp.bfloat16
 F32 = jnp.float32
 VMEM_MB = 60
+GROUPS = ((0, 1), (1, 1), (2, 2))
 
 
 def seat(pair, frame):
@@ -35,9 +36,13 @@
     return (frame >= 0) & (frame < FRAMES)
 
 
+def crosses(frame, there, rel):
+    return (rel < 4) & ((frame >> 2) != (there >> 2))
+
+
 def sent_to(frame, rel):
     there = jnp.where(rel == 6, (frame + 8) & 15, frame + shift_of(rel))
-    return there, inside(there)
+    return there, inside(there) & jnp.logical_not(crosses(frame, there, rel))
 
 
 def came_from(frame, rel):
@@ -47,10 +52,10 @@
 
 def attention_kernel(
     q_in, k_in, v_in, g_in, mask,
-    o_out, dq_out, dk_out, dv_out,
-    rows, kv, qg, scores, gradw, weights, scores_b, parts, back, outs,
+    results,
+    rows, kv, qg, scores, gradw, weights, scores_b, parts, back, onway, outs,
     peak, acc, dq_acc, rowl, rowd, qt, gt, bias,
-    in_sem, s1, r1, s2, r2, s3, r3, s4, r4,
+    in_sem, s1, r1, s2, r2, s3, r3, s4, r4, s5, r6,
 ):
     seq = lax.axis_index("seq")
     plane = lax.axis_index("head")
@@ -65,6 +70,16 @@
     my_head = jnp.where(own_hit, head, -1)
     my_spot = jnp.where(own_hit, src_spot, -1)
     seat0 = seat(0, src_frame)
+    row, col = frame >> 2, frame & 3
+    low = col < 2
+    hub = jnp.where(low, 5, 4)
+    has_hub = jnp.where(low, row < 3, row > 0)
+
+    def passed_to(gap):
+        there = row * 4 + jnp.where(low, 4 + col - gap, col - 4 + gap)
+        ok = has_hub & ((there >> 2) == row)
+        return there, ok, 2 * (gap - 1) + low.astype(jnp.int32)
+
 
     fetch = [
         pltpu.make_async_copy(ref, rows.at[n], in_sem.at[n])
@@ -90,20 +105,16 @@
 
         lax.fori_loop(0, PLANES, greet_owners, 0)
 
-        def greet_partner(rel, carry):
-            there, ok = sent_to(frame, rel)
+        for step in range(1, 4):
+            greet((seat(pair, row * 4 + ((col + step) & 3)), plane))
+        for rel in range(4, UNITS - 1):
+            there, ok = sent_to(frame, jnp.int32(rel))
 
             @pl.when(ok)
-            def _():
+            def _(there=there):
                 greet((seat(pair, there), plane))
 
-            return carry
-
-        lax.fori_loop(0, UNITS - 1, greet_partner, 0)
-
-    partners = jnp.int32(0)
-    for rel in range(UNITS - 1):
-        partners = partners + came_from(frame, jnp.int32(rel))[1].astype(jnp.int32)
+    partners = 4 + (row > 0).astype(jnp.int32) + (row < 3).astype(jnp.int32)
     expected = HEADS + busy.astype(jnp.int32) * partners
     for copy in fetch:
         copy.wait()
@@ -152,34 +163,55 @@
         )
         return copy, ok
 
-    def grad_copy(rel):
-        there, ok = came_from(frame, rel)
+    def pass_on(gap):
+        there, ok, slot = passed_to(gap)
         copy = pltpu.make_async_remote_copy(
-            src_ref=parts.at[rel + 1], dst_ref=back.at[rel], send_sem=s3.at[rel],
-            recv_sem=r3.at[rel],
+            src_ref=kv.at[hub + 1], dst_ref=kv.at[slot + 1], send_sem=s5.at[gap - 1],
+            recv_sem=r2.at[slot],
             device_id=(seat(pair, there), plane), device_id_type=pl.DeviceIdType.MESH,
         )
         return copy, ok
 
-    def give_result(array):
-        dst = (o_out, dq_out, dk_out, dv_out)[array].at[
-            :, pl.ds(pl.multiple_of(head * HD, HD), HD)
-        ]
-
-        def send(z, carry):
+    def grad_start(rel):
+        there, _ = came_from(frame, rel)
+        via = crosses(frame, there, rel)
+
+        @pl.when(via)
+        def _():
+            pltpu.make_async_remote_copy(
+                src_ref=parts.at[rel + 1], dst_ref=onway.at[rel >> 1], send_sem=s3.at[rel],
+                recv_sem=r6.at[rel >> 1],
+                device_id=(seat(pair, row * 4 + (there & 3)), plane),
+                device_id_type=pl.DeviceIdType.MESH,
+            ).start()
+
+        @pl.when(jnp.logical_not(via))
+        def _():
+            pltpu.make_async_remote_copy(
+                src_ref=parts.at[rel + 1], dst_ref=back.at[rel], send_sem=s3.at[rel],
+                recv_sem=r3.at[rel],
+                device_id=(seat(pair, there), plane), device_id_type=pl.DeviceIdType.MESH,
+            ).start()
+
+    def give_result(first, count, sem):
+        arrays = pl.ds(first, count)
+        dst = results.at[arrays, :, pl.ds(pl.multiple_of(head * HD, HD), HD)]
+
+        def send(k, carry):
+            z = (plane + 4 + ((k + 1) >> 1) * (2 * (k & 1) - 1)) & 7
             for r in range(4):
                 spot = r * 8 + z
-                src = outs.at[array, pl.ds(pl.multiple_of(spot * SUB, SUB), SUB), :]
+                src = outs.at[arrays, pl.ds(pl.multiple_of(spot * SUB, SUB), SUB), :]
                 mine = spot == my_spot
 
                 @pl.when(mine)
                 def _(src=src):
-                    pltpu.make_async_copy(src, dst, r4.at[array]).start()
+                    pltpu.make_async_copy(src, dst, r4.at[sem]).start()
 
                 @pl.when(jnp.logical_not(mine))
                 def _(src=src, r=r):
                     pltpu.make_async_remote_copy(
-                        src_ref=src, dst_ref=dst, send_sem=s4.at[array], recv_sem=r4.at[array],
+                        src_ref=src, dst_ref=dst, send_sem=s4.at[sem], recv_sem=r4.at[sem],
                         device_id=(frame * 4 + r, z), device_id_type=pl.DeviceIdType.MESH,
                     ).start()
 
@@ -191,7 +223,8 @@
     def _():
         pltpu.make_async_copy(kv.at[0], kv.at[0], r1.at[0]).wait()
 
-        def send_partner(rel, carry):
+        def send_partner(n, carry):
+            rel = jnp.where(n < 2, n + 4, jnp.where(n < 6, n - 2, 6))
             copy, ok = kv_copy(rel)
 
             @pl.when(ok)
@@ -227,12 +260,23 @@
         def has_unit(u):
             return (u == 0) | came_from(frame, u - 1 + (u == 0).astype(jnp.int32))[1]
 
-        def first_pass(u, carry):
+        def first_pass(n, carry):
+            u = jnp.where(n == 0, 0, jnp.where(n < 3, n + 4, jnp.where(n < 7, n - 2, 7)))
+
             @pl.when(has_unit(u))
             def _():
                 @pl.when(u > 0)
                 def _():
-                    pltpu.make_async_copy(kv.at[u], kv.at[u], r2.at[u - 1]).wait()
+                    wait_for(kv.at[u], r2.at[u - 1])
+
+                @pl.when(u == hub + 1)
+                def _():
+                    for gap in (1, 2):
+                        copy, ok = pass_on(gap)
+
+                        @pl.when(ok)
+                        def _(copy=copy):
+                            copy.start()
 
                 keys = kv[u, 0]
                 values = kv[u, 1]
@@ -275,7 +319,7 @@
         inv = 1.0 / jnp.sum(rowl[...], axis=1, keepdims=True)
         attended = (acc[...] * inv).astype(BF)
         outs[0] = attended
-        give_result(0)
+        give_result(0, 1, 0)
         grads = qg[1].astype(F32)
         delta = jnp.sum(grads * attended.astype(F32), axis=1, keepdims=True)
         gt[...] = (grads * inv).astype(BF).T
@@ -284,7 +328,17 @@
         rowd[...] = jnp.broadcast_to(inv * delta, (FT, HD))
 
         def third_pass(n, carry):
-            u = UNITS - 1 - n
+            near = jnp.where(low, 1, 2)
+            u = jnp.where(
+                n < 2, near + 2 * n,
+                jnp.where(
+                    n == 2, 7,
+                    jnp.where(
+                        n == 3, 10 - hub,
+                        jnp.where(n == 4, hub + 1, jnp.where(n < 7, 3 - near + 2 * (n - 5), 0)),
+                    ),
+                ),
+            )
 
             @pl.when(has_unit(u))
             def _():
@@ -298,9 +352,21 @@
                 parts[u, 0] = jnp.dot(qt[...], ds, preferred_element_type=F32).astype(BF)
                 parts[u, 1] = jnp.dot(gt[...], weights[u], preferred_element_type=F32).astype(BF)
 
+                @pl.when(u == hub + 1)
+                def _():
+                    for gap in (1, 2):
+
+                        @pl.when(passed_to(gap)[1])
+                        def _(gap=gap):
+                            wait_for(onway.at[gap - 1], r6.at[gap - 1])
+                            for n in range(2):
+                                parts[u, n] = (
+                                    parts[u, n].astype(F32) + onway[gap - 1, n].astype(F32)
+                                ).astype(BF)
+
                 @pl.when(u > 0)
                 def _():
-                    grad_copy(u - 1)[0].start()
+                    grad_start(u - 1)
 
                 dq_acc[...] += jnp.dot(ds, kv[u, 0], preferred_element_type=F32)
 
@@ -308,7 +374,7 @@
 
         lax.fori_loop(0, UNITS, third_pass, 0)
         outs[1] = dq_acc[...].astype(BF)
-        give_result(1)
+        give_result(1, 1, 1)
 
         sums = scores.at[0, pl.ds(0, 256)]
         sums[0:128] = parts[0, 0].astype(F32)
@@ -325,9 +391,8 @@
 
         lax.fori_loop(0, UNITS - 1, add_back, 0)
         outs[2] = sums[0:128].T.astype(BF)
-        give_result(2)
         outs[3] = sums[128:256].T.astype(BF)
-        give_result(3)
+        give_result(2, 2, 2)
 
         def partner_sent(rel, carry):
             copy, ok = kv_copy(rel)
@@ -336,24 +401,30 @@
             def _():
                 copy.wait_send()
 
-            copy, ok = grad_copy(rel)
+            @pl.when(came_from(frame, rel)[1])
+            def _():
+                wait_for(parts.at[rel + 1], s3.at[rel])
+
+            return carry
+
+        lax.fori_loop(0, UNITS - 1, partner_sent, 0)
+        for gap in (1, 2):
+            copy, ok = pass_on(gap)
 
             @pl.when(ok)
-            def _():
+            def _(copy=copy):
                 copy.wait_send()
 
-            return carry
-
-        lax.fori_loop(0, UNITS - 1, partner_sent, 0)
-        for array in range(4):
+        for sem, (first, count) in enumerate(GROUPS):
+            given = outs.at[pl.ds(first, count)]
 
             @pl.when(own_hit)
-            def _(array=array):
-                wait_for(outs.at[array, pl.ds(0, FT - SUB)], s4.at[array])
+            def _(given=given, sem=sem):
+                wait_for(given.at[:, pl.ds(0, FT - SUB)], s4.at[sem])
 
             @pl.when(jnp.logical_not(own_hit))
-            def _(array=array):
-                wait_for(outs.at[array], s4.at[array])
+            def _(given=given, sem=sem):
+                wait_for(given, s4.at[sem])
 
     for stage in range(2):
         sent = rows.at[pl.ds(2 * stage, 2)]
@@ -366,19 +437,19 @@
         def _(sent=sent, stage=stage):
             wait_for(sent, s1.at[stage])
 
-    for n, ref in enumerate((o_out, dq_out, dk_out, dv_out)):
-        pltpu.make_async_copy(ref, ref, r4.at[n]).wait()
+    for sem, (first, count) in enumerate(GROUPS):
+        wait_for(results.at[pl.ds(first, count)], r4.at[sem])
 
 
 def per_device(query_rows, key_rows, value_rows, out_grad, block_mask):
     anywhere = pl.BlockSpec(memory_space=pl.ANY)
     result = jax.ShapeDtypeStruct(query_rows.shape, BF)
     dma = pltpu.SemaphoreType.DMA
-    return pl.pallas_call(
+    results = pl.pallas_call(
         attention_kernel,
-        out_shape=(result,) * 4,
+        out_shape=jax.ShapeDtypeStruct((4,) + query_rows.shape, BF),
         in_specs=[anywhere] * 4 + [pl.BlockSpec(memory_space=pltpu.SMEM)],
-        out_specs=(anywhere,) * 4,
+        out_specs=anywhere,
         scratch_shapes=[
             pltpu.VMEM((4, SUB, HEADS * HD), BF),
             pltpu.VMEM((UNITS, 2, FT, HD), BF),
@@ -389,6 +460,7 @@
             pltpu.VMEM((UNITS, FT, FT), BF),
             pltpu.VMEM((UNITS, 2, HD, FT), BF),
             pltpu.VMEM((UNITS - 1, 2, HD, FT), BF),
+            pltpu.VMEM((2, 2, HD, FT), BF),
             pltpu.VMEM((4, FT, HD), BF),
             pltpu.VMEM((FT, HD), F32),
             pltpu.VMEM((FT, HD), F32),
@@ -405,13 +477,16 @@
             dma((UNITS - 1,)),
             dma((UNITS - 1,)),
             dma((UNITS - 1,)),
-            dma((4,)),
-            dma((4,)),
+            dma((3,)),
+            dma((3,)),
+            dma((2,)),
+            dma((2,)),
         ],
         compiler_params=pltpu.CompilerParams(
             collective_id=0, has_side_effects=True, vmem_limit_bytes=VMEM_MB * 1024 * 1024
         ),
     )(query_rows, key_rows, value_rows, out_grad, block_mask)
+    return tuple(results[n] for n in range(4))
 
 
 def solution(mesh):

time: 82.4 us -> 74 us (0.90)
  the two profiles are of different devices: /device:TPU:3 before, /device:TPU:17 now
where the time goes in v3:
time: 74 us; the launch traced here: 73.8 us
  Pallas kernels  71.4 us (96%)
  local copies, waits for them, and re-layouts  1.78 us (2%)
    pallas_call x1, Pallas kernels, per_device(): pl.pallas_call(attention_kernel, out_shape=jax.ShapeDtypeStruct((4,) + qu...  71.4 us
    squeeze x1, local copies, waits for them, and re-layouts, per_device(): return tuple((results[n] for n in range(4)))  1.78 us

profile of v3, /device:TPU:17, one launch (start us, length us, event | category | flops | bytes accessed | tf_op | source)
XLA Modules:
  0.0 73.8 jit_solution(15732905205297727512)
XLA Ops:
  0.6 71.4 %shard_map.84 = bf16[4,16,3072]{2,1,0:T(8,128)(2,1)} custom-call(bf16[16,3072]{1,0:T(8,128)(2,1)} %q_in.1, bf16[16,3072]{1,0:T(8,128)(2,1)} %k_in.1, bf16[16,3072]{1,0:T(8,128)(2,1)} %v_in.1, bf16[16,3072]{1,0:T(8,128)(2,1)} %g_in.1, s32[4,4,4]{2,1,0:T(4,128)} %mask.1), custom_call_target="tpu_custom_call" | custom-call | tf_op jit(solution)/shard_map/pallas_call | solution.py:448
  72.0 1.8 %slice_bitcast_fusion = (bf16[16,3072]{1,0:T(8,128)(2,1)}, bf16[16,3072]{1,0:T(8,128)(2,1)}, bf16[16,3072]{1,0:T(8,128)(2,1)}, bf16[16,3072]{1,0:T(8,128)(2,1)}) fusion(bf16[4,16,3072]{2,1,0:T(8,128)(2,1)} %shard_map.84), kind=kLoop, calls=%fused_computation | loop fusion | bytes 786432 | tf_op jit(solution)/shard_map/squeeze | solution.py:489

commit v4 on v3

--- a/solution.py
+++ b/solution.py
@@ -30,6 +30,12 @@
 
 def shift_of(rel):
     return (1 - 2 * (rel & 1)) * lax.shift_left(jnp.int32(1), rel >> 1)
+
+
+def order(steps, n):
+    return lax.shift_right_logical(
+        jnp.int32(sum(step << (3 * k) for k, step in enumerate(steps))), 3 * n
+    ) & 7
 
 
 def inside(frame):
@@ -172,15 +178,22 @@
         )
         return copy, ok
 
+    def share():
+        return pltpu.make_async_remote_copy(
+            src_ref=kv.at[2], dst_ref=kv.at[1], send_sem=s5.at[2], recv_sem=r2.at[0],
+            device_id=(seat(pair, frame + 2), plane), device_id_type=pl.DeviceIdType.MESH,
+        )
+
     def grad_start(rel):
         there, _ = came_from(frame, rel)
         via = crosses(frame, there, rel)
+        spot = rel >> 1
 
         @pl.when(via)
         def _():
             pltpu.make_async_remote_copy(
-                src_ref=parts.at[rel + 1], dst_ref=onway.at[rel >> 1], send_sem=s3.at[rel],
-                recv_sem=r6.at[rel >> 1],
+                src_ref=parts.at[rel + 1], dst_ref=onway.at[spot], send_sem=s3.at[rel],
+                recv_sem=r6.at[spot],
                 device_id=(seat(pair, row * 4 + (there & 3)), plane),
                 device_id_type=pl.DeviceIdType.MESH,
             ).start()
@@ -197,8 +210,7 @@
         arrays = pl.ds(first, count)
         dst = results.at[arrays, :, pl.ds(pl.multiple_of(head * HD, HD), HD)]
 
-        def send(k, carry):
-            z = (plane + 4 + ((k + 1) >> 1) * (2 * (k & 1) - 1)) & 7
+        def send(z, carry):
             for r in range(4):
                 spot = r * 8 + z
                 src = outs.at[arrays, pl.ds(pl.multiple_of(spot * SUB, SUB), SUB), :]
@@ -224,10 +236,10 @@
         pltpu.make_async_copy(kv.at[0], kv.at[0], r1.at[0]).wait()
 
         def send_partner(n, carry):
-            rel = jnp.where(n < 2, n + 4, jnp.where(n < 6, n - 2, 6))
+            rel = order((4, 5, 1, 0, 2, 3, 6), n)
             copy, ok = kv_copy(rel)
 
-            @pl.when(ok)
+            @pl.when(ok & ((rel > 0) | (col == 0)))
             def _():
                 copy.start()
 
@@ -261,13 +273,19 @@
             return (u == 0) | came_from(frame, u - 1 + (u == 0).astype(jnp.int32))[1]
 
         def first_pass(n, carry):
-            u = jnp.where(n == 0, 0, jnp.where(n < 3, n + 4, jnp.where(n < 7, n - 2, 7)))
+            u = jnp.where(
+                low, order((0, 6, 2, 5, 1, 3, 4, 7), n), order((0, 5, 6, 2, 3, 4, 1, 7), n)
+            )
 
             @pl.when(has_unit(u))
             def _():
                 @pl.when(u > 0)
                 def _():
                     wait_for(kv.at[u], r2.at[u - 1])
+
+                @pl.when(low & (u == 2))
+                def _():
+                    share().start()
 
                 @pl.when(u == hub + 1)
                 def _():
@@ -327,17 +345,14 @@
         rowl[...] = jnp.broadcast_to(inv, (FT, HD))
         rowd[...] = jnp.broadcast_to(inv * delta, (FT, HD))
 
+        def collect(u, spot):
+            wait_for(onway.at[spot], r6.at[spot])
+            for n in range(2):
+                parts[u, n] = (parts[u, n].astype(F32) + onway[spot, n].astype(F32)).astype(BF)
+
         def third_pass(n, carry):
-            near = jnp.where(low, 1, 2)
             u = jnp.where(
-                n < 2, near + 2 * n,
-                jnp.where(
-                    n == 2, 7,
-                    jnp.where(
-                        n == 3, 10 - hub,
-                        jnp.where(n == 4, hub + 1, jnp.where(n < 7, 3 - near + 2 * (n - 5), 0)),
-                    ),
-                ),
+                low, order((1, 3, 7, 5, 6, 2, 4, 0), n), order((2, 4, 7, 6, 5, 1, 3, 0), n)
             )
 
             @pl.when(has_unit(u))
@@ -358,11 +373,8 @@
 
                         @pl.when(passed_to(gap)[1])
                         def _(gap=gap):
-                            wait_for(onway.at[gap - 1], r6.at[gap - 1])
-                            for n in range(2):
-                                parts[u, n] = (
-                                    parts[u, n].astype(F32) + onway[gap - 1, n].astype(F32)
-                                ).astype(BF)
+                            collect(u, gap - 1)
+
 
                 @pl.when(u > 0)
                 def _():
@@ -397,7 +409,7 @@
         def partner_sent(rel, carry):
             copy, ok = kv_copy(rel)
 
-            @pl.when(ok)
+            @pl.when(ok & ((rel > 0) | (col == 0)))
             def _():
                 copy.wait_send()
 
@@ -414,6 +426,10 @@
             @pl.when(ok)
             def _(copy=copy):
                 copy.wait_send()
+
+        @pl.when(low)
+        def _():
+            share().wait_send()
 
         for sem, (first, count) in enumerate(GROUPS):
             given = outs.at[pl.ds(first, count)]
@@ -479,7 +495,7 @@
             dma((UNITS - 1,)),
             dma((3,)),
             dma((3,)),
-            dma((2,)),
+            dma((3,)),
             dma((2,)),
         ],
         compiler_params=pltpu.CompilerParams(

time: 74 us -> 73.4 us (level)
  no operation moved by 1% of the time
where the time goes in v4:
time: 73.4 us; the launch traced here: 73.2 us
  Pallas kernels  70.7 us (96%)
  local copies, waits for them, and re-layouts  1.78 us (2%)
    pallas_call x1, Pallas kernels, per_device(): pl.pallas_call(attention_kernel, out_shape=jax.ShapeDtypeStruct((4,) + qu...  70.7 us
    squeeze x1, local copies, waits for them, and re-layouts, per_device(): return tuple((results[n] for n in range(4)))  1.78 us

profile of v4, /device:TPU:17, one launch (start us, length us, event | category | flops | bytes accessed | tf_op | source)
XLA Modules:
  0.0 73.2 jit_solution(9959750249190078241)
XLA Ops:
  0.6 70.7 %shard_map.84 = bf16[4,16,3072]{2,1,0:T(8,128)(2,1)} custom-call(bf16[16,3072]{1,0:T(8,128)(2,1)} %q_in.1, bf16[16,3072]{1,0:T(8,128)(2,1)} %k_in.1, bf16[16,3072]{1,0:T(8,128)(2,1)} %v_in.1, bf16[16,3072]{1,0:T(8,128)(2,1)} %g_in.1, s32[4,4,4]{2,1,0:T(4,128)} %mask.1), custom_call_target="tpu_custom_call" | custom-call | tf_op jit(solution)/shard_map/pallas_call | solution.py:464
  71.4 1.8 %slice_bitcast_fusion = (bf16[16,3072]{1,0:T(8,128)(2,1)}, bf16[16,3072]{1,0:T(8,128)(2,1)}, bf16[16,3072]{1,0:T(8,128)(2,1)}, bf16[16,3072]{1,0:T(8,128)(2,1)}) fusion(bf16[4,16,3072]{2,1,0:T(8,128)(2,1)} %shard_map.84), kind=kLoop, calls=%fused_computation | loop fusion | bytes 786432 | tf_op jit(solution)/shard_map/squeeze | solution.py:505

commit v5 on v4

--- a/solution.py
+++ b/solution.py
@@ -91,9 +91,6 @@
         pltpu.make_async_copy(ref, rows.at[n], in_sem.at[n])
         for n, ref in enumerate((k_in, v_in, q_in, g_in))
     ]
-    for copy in fetch:
-        copy.start()
-
     barrier = pltpu.get_barrier_semaphore()
 
     def greet(target):
@@ -119,6 +116,9 @@
             @pl.when(ok)
             def _(there=there):
                 greet((seat(pair, there), plane))
+
+    for copy in fetch:
+        copy.start()
 
     partners = 4 + (row > 0).astype(jnp.int32) + (row < 3).astype(jnp.int32)
     expected = HEADS + busy.astype(jnp.int32) * partners
@@ -352,7 +352,7 @@
 
         def third_pass(n, carry):
             u = jnp.where(
-                low, order((1, 3, 7, 5, 6, 2, 4, 0), n), order((2, 4, 7, 6, 5, 1, 3, 0), n)
+                low, order((1, 3, 5, 7, 6, 2, 4, 0), n), order((2, 4, 6, 7, 5, 1, 3, 0), n)
             )
 
             @pl.when(has_unit(u))
@@ -392,7 +392,9 @@
         sums[0:128] = parts[0, 0].astype(F32)
         sums[128:256] = parts[0, 1].astype(F32)
 
-        def add_back(rel, carry):
+        def add_back(n, carry):
+            rel = order((6, 0, 1, 2, 3, 4, 5), n)
+
             @pl.when(sent_to(frame, rel)[1])
             def _():
                 pltpu.make_async_copy(back.at[rel], back.at[rel], r3.at[rel]).wait()

time: 73.4 us -> 73.4 us (level)
  no operation moved by 1% of the time
where the time goes in v5:
time: 73.4 us; the launch traced here: 73.2 us
  Pallas kernels  70.7 us (96%)
  local copies, waits for them, and re-layouts  1.78 us (2%)
    pallas_call x1, Pallas kernels, per_device(): pl.pallas_call(attention_kernel, out_shape=jax.ShapeDtypeStruct((4,) + qu...  70.7 us
    squeeze x1, local copies, waits for them, and re-layouts, per_device(): return tuple((results[n] for n in range(4)))  1.78 us

profile of v5, /device:TPU:17, one launch (start us, length us, event | category | flops | bytes accessed | tf_op | source)
XLA Modules:
  0.0 73.2 jit_solution(3500622413209272386)
XLA Ops:
  0.6 70.7 %shard_map.84 = bf16[4,16,3072]{2,1,0:T(8,128)(2,1)} custom-call(bf16[16,3072]{1,0:T(8,128)(2,1)} %q_in.1, bf16[16,3072]{1,0:T(8,128)(2,1)} %k_in.1, bf16[16,3072]{1,0:T(8,128)(2,1)} %v_in.1, bf16[16,3072]{1,0:T(8,128)(2,1)} %g_in.1, s32[4,4,4]{2,1,0:T(4,128)} %mask.1), custom_call_target="tpu_custom_call" | custom-call | tf_op jit(solution)/shard_map/pallas_call | solution.py:466
  71.4 1.8 %slice_bitcast_fusion = (bf16[16,3072]{1,0:T(8,128)(2,1)}, bf16[16,3072]{1,0:T(8,128)(2,1)}, bf16[16,3072]{1,0:T(8,128)(2,1)}, bf16[16,3072]{1,0:T(8,128)(2,1)}) fusion(bf16[4,16,3072]{2,1,0:T(8,128)(2,1)} %shard_map.84), kind=kLoop, calls=%fused_computation | loop fusion | bytes 786432 | tf_op jit(solution)/shard_map/squeeze | solution.py:507
